TPU v7x, 128 devices: a whole 4x4x4 slice. The times are simulated.
128 devices in a mesh: dp: 16 (over y, z), mp: 8 (over x, core).
Axes of the slice: x: 4, y: 4, z: 4, core: 2. Of those that a mesh axis runs over, the one named last changes fastest.
Arguments:
- hidden_in: bfloat16 [4096, 2304], P('dp'), may hold values from -6 to 6
- attn_gain: float32 [2304], replicated, may hold values from 0.25 to 1.75
- w_query: bfloat16 [2304, 2048], P(None, 'mp'), may hold values from -0.25 to 0.25
- w_key: bfloat16 [2304, 2048], P(None, 'mp'), may hold values from -0.125 to 0.125
- w_value: bfloat16 [2304, 2048], P(None, 'mp'), may hold values from -0.125 to 0.125
- w_out: bfloat16 [2048, 2304], P('mp'), may hold values from -0.5 to 0.5
- root_cache: bfloat16 [2, 4096, 2048], P(None, 'dp', 'mp'), may hold values from -400 to 400
- mid_cache: bfloat16 [2, 16, 1024, 2048], P(None, 'dp', None, 'mp'), may hold values from -400 to 400
- leaf_cache: bfloat16 [2, 32, 1024, 2048], P(None, 'dp', None, 'mp'), may hold values from -400 to 400
- mid_len: int32 [16], P('dp'), may hold values from 1 to 1024, 8192 in all
- leaf_len: int32 [32], P('dp'), may hold values from 1 to 1024, 16384 in all
- leaf_of: int32 [128], P('dp'), may hold values from 0 to 31, as said below
- parents: int32 [32], replicated, may hold values from 0 to 15, as said below
- suffix_len: int32 [128], P('dp'), may hold values from 1 to 32, 3072 in all
- ffn_gain: float32 [2304], replicated, may hold values from 0.25 to 1.75
- w_router: float32 [2304, 8], replicated, may hold values from -0.5 to 0.5
- routes: int32 [4096, 2], P('dp'), may hold values from 0 to 7, all different within a row; in each aligned block of 256 rows (0 to 255, 256 to 511, ...) at most 96 rows name the same one
- w_gate: bfloat16 [8, 2304, 5760], P('mp', None, 'dp'), may hold values from -0.125 to 0.125
- w_up: bfloat16 [8, 2304, 5760], P('mp', None, 'dp'), may hold values from -0.125 to 0.125
- w_down: bfloat16 [8, 5760, 2304], P('mp', 'dp'), may hold values from -0.078125 to 0.078125
Outputs:
- layer_out: bfloat16 [4096, 2304], P(('dp', 'mp'))
Inputs may be any that keep to these rules, and one draw needn't show every extreme that they name: `leaf_of`: leaf n belongs to index n // 2 of dp, mid-level node n to index n. The 8 sequences of one index of dp have different mid-level nodes and leaves of one parity, so that no two of them share a mid-level node or a leaf's owner. `parents`: every mid-level node is the parent of exactly one even and one odd leaf. `routes`: in the rows of one index of dp no expert is named by more than 96 rows; some indices of dp reach 96.
All inputs are finite; a program needn't handle non-finite values. No bound on the sum of `mid_len` or of `leaf_len` or of `suffix_len` on one device may be relied on, other than what follows from the above.
Results may differ from a plain program's by a relative error of at most 0.015.
The roundings to bfloat16 on the way count: a program that leaves them out, or rounds other values in their place, can miss the bound.
Values may be sent and summed in bfloat16 or wider, within the bound.
A program may use at most 128 MiB of HBM per device.

v0:
```python
import math

import jax
import jax.numpy as jnp
from jax import lax
from jax.sharding import PartitionSpec as P

HD = 64
TOP = 2


EPS = 1e-05
NEGATIVE = -1e30


def rms_scale(rows, gain):
    rows_wide = rows.astype(jnp.float32)
    mean_square = jnp.mean(rows_wide * rows_wide, axis=-1, keepdims=True)
    return rows_wide * lax.rsqrt(mean_square + EPS) * gain


def level_partial(queries, node_keys, node_values, limits, heads_here, batched):
    senders, row_count, width = queries.shape
    head_dim = width // heads_here
    scale = 1.0 / math.sqrt(head_dim)
    query_heads = queries.reshape(senders, row_count, heads_here, head_dim)
    if batched:
        key_heads = node_keys.reshape(senders, -1, heads_here, head_dim)
        value_heads = node_values.reshape(senders, -1, heads_here, head_dim)
        scores = jnp.einsum(
            "sqhd,skhd->sqhk", query_heads, key_heads, preferred_element_type=jnp.float32
        )
    else:
        key_heads = node_keys.reshape(-1, heads_here, head_dim)
        value_heads = node_values.reshape(-1, heads_here, head_dim)
        scores = jnp.einsum(
            "sqhd,khd->sqhk", query_heads, key_heads, preferred_element_type=jnp.float32
        )
    scores = scores * scale
    slots = jnp.arange(scores.shape[-1], dtype=jnp.int32)
    allowed = slots[None, :] < limits[:, None]
    scores = jnp.where(allowed[:, None, None, :], scores, NEGATIVE)
    peak = jnp.max(scores, axis=-1)
    weights = jnp.exp(scores - peak[..., None])
    total = jnp.sum(weights, axis=-1)
    probs = weights.astype(jnp.bfloat16)
    if batched:
        summed = jnp.einsum(
            "sqhk,skhd->sqhd", probs, value_heads, preferred_element_type=jnp.float32
        )
    else:
        summed = jnp.einsum(
            "sqhk,khd->sqhd", probs, value_heads, preferred_element_type=jnp.float32
        )
    result = (summed / total[..., None]).reshape(senders, row_count, width)
    return (result, peak + jnp.log(total))


def on_device(
    hidden_in,
    attn_gain,
    w_query,
    w_key,
    w_value,
    w_out,
    root_cache,
    mid_cache,
    leaf_cache,
    mid_len,
    leaf_len,
    leaf_of,
    parents,
    suffix_len,
    ffn_gain,
    w_router,
    routes,
    w_gate,
    w_up,
    w_down,
):
    tok_rows, width = hidden_in.shape
    seq_rows = suffix_len.shape[0]
    suffix = tok_rows // seq_rows
    head_dim = HD
    local_width = w_query.shape[1]
    heads_here = local_width // head_dim
    scale = 1.0 / math.sqrt(head_dim)
    owners = lax.axis_size("dp")
    normed = rms_scale(hidden_in, attn_gain).astype(jnp.bfloat16)
    query = jnp.dot(normed, w_query, preferred_element_type=jnp.float32).astype(jnp.bfloat16)
    key = jnp.dot(normed, w_key, preferred_element_type=jnp.float32).astype(jnp.bfloat16)
    value = jnp.dot(normed, w_value, preferred_element_type=jnp.float32).astype(jnp.bfloat16)
    query_heads = query.reshape(tok_rows, heads_here, head_dim)
    piece = lax.all_gather(root_cache, "dp", axis=1, tiled=True)
    running_peak = jnp.full((tok_rows, heads_here), NEGATIVE, jnp.float32)
    piece_keys = piece[0].reshape(-1, heads_here, head_dim)
    piece_values = piece[1].reshape(-1, heads_here, head_dim)
    scores = (
        jnp.einsum("qhd,khd->qhk", query_heads, piece_keys, preferred_element_type=jnp.float32)
        * scale
    )
    new_peak = jnp.maximum(running_peak, jnp.max(scores, axis=-1))
    weights = jnp.exp(scores - new_peak[..., None])
    new_total = jnp.sum(weights, axis=-1)
    added = jnp.einsum(
        "qhk,khd->qhd",
        weights.astype(jnp.bfloat16),
        piece_values,
        preferred_element_type=jnp.float32,
    )
    root_out = added / new_total[..., None]
    root_lse = new_peak + jnp.log(new_total)
    query_seq = query.reshape(seq_rows, suffix, heads_here, head_dim)
    key_seq = key.reshape(seq_rows, suffix, heads_here, head_dim)
    value_seq = value.reshape(seq_rows, suffix, heads_here, head_dim)
    slots = jnp.arange(suffix, dtype=jnp.int32)
    self_ok = (slots[None, None, :] <= slots[None, :, None]) & (
        slots[None, None, :] < suffix_len[:, None, None]
    )
    self_scores = (
        jnp.einsum("sqhd,skhd->sqhk", query_seq, key_seq, preferred_element_type=jnp.float32)
        * scale
    )
    self_scores = jnp.where(self_ok[:, :, None, :], self_scores, NEGATIVE)
    self_peak = jnp.max(self_scores, axis=-1)
    self_weights = jnp.exp(self_scores - self_peak[..., None])
    self_total = jnp.sum(self_weights, axis=-1)
    self_sum = jnp.einsum(
        "sqhk,skhd->sqhd",
        self_weights.astype(jnp.bfloat16),
        value_seq,
        preferred_element_type=jnp.float32,
    )
    self_out = (self_sum / self_total[..., None]).reshape(tok_rows, heads_here, head_dim)
    self_lse = (self_peak + jnp.log(self_total)).reshape(tok_rows, heads_here)
    mid_of = parents[leaf_of]
    leaf_owner = leaf_of // 2
    leaf_side = (leaf_of % 2).astype(jnp.float32)
    targets = jnp.arange(owners, dtype=jnp.int32)
    pick_mid = (mid_of[None, :] == targets[:, None]).astype(jnp.bfloat16)
    pick_leaf = (leaf_owner[None, :] == targets[:, None]).astype(jnp.bfloat16)
    flat_query = query.reshape(seq_rows, suffix * local_width)
    sent_mid = jnp.dot(pick_mid, flat_query, preferred_element_type=jnp.float32).astype(
        jnp.bfloat16
    )
    sent_leaf = jnp.dot(pick_leaf, flat_query, preferred_element_type=jnp.float32).astype(
        jnp.bfloat16
    )
    sent = jnp.stack([sent_mid, sent_leaf], axis=1).reshape(owners, 2, suffix, local_width)
    side_of_target = jnp.dot(
        pick_leaf.astype(jnp.float32), leaf_side, precision=lax.Precision.HIGHEST
    )
    sides = jnp.stack([jnp.zeros_like(side_of_target), side_of_target], axis=1)
    sides = jnp.broadcast_to(sides[:, :, None], (owners, 2, suffix)).astype(jnp.bfloat16)
    sent_queries = lax.all_to_all(sent, "dp", split_axis=0, concat_axis=0, tiled=True)
    sent_sides = lax.all_to_all(sides, "dp", split_axis=0, concat_axis=0, tiled=True)
    senders = sent_queries.shape[0]
    second = sent_sides[:, 1, 0] > 0.5
    mid_limit = jnp.broadcast_to(mid_len[0], (senders,))
    mid_result, mid_logsum = level_partial(
        sent_queries[:, 0], mid_cache[0, 0], mid_cache[1, 0], mid_limit, heads_here, False
    )
    leaf_keys = jnp.where(second[:, None, None], leaf_cache[0, 1][None], leaf_cache[0, 0][None])
    leaf_values = jnp.where(second[:, None, None], leaf_cache[1, 1][None], leaf_cache[1, 0][None])
    leaf_limit = jnp.where(second, leaf_len[1], leaf_len[0])
    leaf_result, leaf_logsum = level_partial(
        sent_queries[:, 1], leaf_keys, leaf_values, leaf_limit, heads_here, True
    )
    owner_out = jnp.stack([mid_result, leaf_result], axis=1)
    owner_lse = jnp.stack([mid_logsum, leaf_logsum], axis=1)
    back_out, back_lse = (
        lax.all_to_all(owner_out, "dp", split_axis=0, concat_axis=0, tiled=True),
        lax.all_to_all(owner_lse, "dp", split_axis=0, concat_axis=0, tiled=True),
    )
    mid_out = back_out[mid_of, 0].reshape(tok_rows, heads_here, head_dim)
    mid_lse = back_lse[mid_of, 0].reshape(tok_rows, heads_here)
    leaf_out = back_out[leaf_owner, 1].reshape(tok_rows, heads_here, head_dim)
    leaf_lse = back_lse[leaf_owner, 1].reshape(tok_rows, heads_here)
    stacked_lse = jnp.stack([root_lse, mid_lse, leaf_lse, self_lse])
    stacked_out = jnp.stack([root_out, mid_out, leaf_out, self_out])
    overall = jnp.max(stacked_lse, axis=0)
    shares = jnp.exp(stacked_lse - overall)
    combined = jnp.sum(shares[..., None] * stacked_out, axis=0) / jnp.sum(shares, axis=0)[..., None]
    attended = combined.reshape(tok_rows, local_width).astype(jnp.bfloat16)
    projected = jnp.dot(attended, w_out, preferred_element_type=jnp.float32)
    rows_here = tok_rows // lax.axis_size("mp")
    first = lax.axis_index("mp") * rows_here
    attn_all = lax.psum(projected, "mp")
    resid_all = hidden_in.astype(jnp.float32) + attn_all
    ffn_in = rms_scale(resid_all, ffn_gain).astype(jnp.bfloat16)
    resid = lax.dynamic_slice_in_dim(resid_all, first, rows_here, 0)
    logits = jnp.dot(ffn_in.astype(jnp.float32), w_router, precision=lax.Precision.HIGHEST)
    chosen = jnp.take_along_axis(logits, routes, axis=1)
    squashed = jax.nn.sigmoid(chosen)
    gates = squashed / jnp.sum(squashed, axis=1, keepdims=True)
    expert = lax.axis_index("mp")
    hit_each = routes == expert
    hit = jnp.any(hit_each, axis=1)
    gate_here = jnp.sum(jnp.where(hit_each, gates, 0.0), axis=1)
    order = jnp.cumsum(hit.astype(jnp.int32)) - 1
    capacity = 3 * TOP * tok_rows // (2 * lax.axis_size("mp"))
    slot_ids = jnp.arange(capacity, dtype=jnp.int32)
    pick_slot = (order[None, :] == slot_ids[:, None]) & hit[None, :]
    dispatch = jnp.dot(
        pick_slot.astype(jnp.bfloat16), ffn_in, preferred_element_type=jnp.float32
    ).astype(jnp.bfloat16)
    slot_gate = jnp.dot(pick_slot.astype(jnp.float32), gate_here, precision=lax.Precision.HIGHEST)
    gate_weight = w_gate[0]
    up_weight = w_up[0]
    down_weight = w_down[0]
    piece = lax.all_gather(dispatch, "dp", axis=0, tiled=True)
    gate_part = jnp.dot(piece, gate_weight, preferred_element_type=jnp.float32)
    up_part = jnp.dot(piece, up_weight, preferred_element_type=jnp.float32)
    partial_out = jnp.dot(
        (jax.nn.silu(gate_part) * up_part).astype(jnp.bfloat16),
        down_weight,
        preferred_element_type=jnp.float32,
    )
    expert_out = lax.psum_scatter(partial_out, "dp", scatter_dimension=0, tiled=True)
    weighted = expert_out * slot_gate[:, None]
    spread = jnp.dot(pick_slot.astype(jnp.float32).T, weighted, precision=lax.Precision.HIGHEST)
    mixed = lax.psum_scatter(spread, "mp", scatter_dimension=0, tiled=True)
    row_ids = first + jnp.arange(rows_here, dtype=jnp.int32)
    valid = row_ids % suffix < suffix_len[row_ids // suffix]
    return jnp.where(valid[:, None], resid + mixed, 0.0).astype(jnp.bfloat16)


def solution(mesh):
    return jax.shard_map(
        on_device,
        mesh=mesh,
        in_specs=(
            P("dp", None),
            P(),
            P(None, "mp"),
            P(None, "mp"),
            P(None, "mp"),
            P("mp", None),
            P(None, "dp", "mp"),
            P(None, "dp", None, "mp"),
            P(None, "dp", None, "mp"),
            P("dp"),
            P("dp"),
            P("dp"),
            P(),
            P("dp"),
            P(),
            P(),
            P("dp", None),
            P("mp", None, "dp"),
            P("mp", None, "dp"),
            P("mp", "dp", None),
        ),
        out_specs=P(("dp", "mp"), None),
        check_vma=False,
    )
```

profile of v0, /device:TPU:1, one launch (start us, length us, event | category | flops | bytes accessed | tf_op | source)
XLA Modules:
  0.0 480.0 jit_solution(8950069300431746591)
XLA Ops:
  9.6 8.6 %all-to-all-start.1 = ((bf16[16,2,32]{2,1,0:T(2,128)(2,1)}), bf16[16,2,32]{2,1,0:T(2,128)(2,1)S(1)}, u32[]{:S(2)}, u32[]{:S(2)}) async-start(bf16[16,2,32]{2,1,0:T(2,128)(2,1)} %broadcast_in_dim.168), calls=%async_computation.1 | async-start | bytes 16384 | tf_op jit(solution)/shard_map/all_to_all | solution.py:156
  18.2 1.6 fusion.30
  19.8 2.5 convolution_convert_fusion.5
  23.4 1.8 convolution_convert_fusion.4
  28.4 1.3 fusion.138
  31.2 1.0 fusion.135
  32.3 1.4 fusion.134
  35.0 7.1 %all-to-all-start = ((bf16[16,2,32,256]{3,2,1,0:T(8,128)(2,1)}), bf16[16,2,32,256]{3,2,1,0:T(8,128)(2,1)}, u32[]{:S(2)}, u32[]{:S(2)}) async-start(bf16[16,2,32,256]{3,2,1,0:T(8,128)(2,1)} %pad_maximum_fusion.1), calls=%async_computation | async-start | bytes 1048576 | tf_op jit(solution)/shard_map/all_to_all | solution.py:155
  42.0 1.2 copy.251
  43.3 2.1 copy.270
  45.4 2.0 copy.290
  47.5 2.0 copy.289
  49.5 2.0 copy.288
  51.6 2.0 copy.291
  54.5 1.6 fusion.97
  56.2 1.9 fusion.136
  58.1 2.0 reshape_squeeze.19
  60.2 2.0 reshape_squeeze.21
  62.2 4.5 bitcast_reduce_fusion.1
  66.8 2.2 fusion.16
  69.0 2.7 fusion.64
  71.7 1.7 copy.274
  73.4 2.6 stack_reshape.25
  76.0 2.4 bitcast_reduce_fusion.2
  78.5 2.6 fusion.14
  82.4 1.5 reshape.482
  83.9 4.5 fusion.69
  88.4 1.7 copy.271
  90.1 2.7 stack_reshape.24
  92.7 6.8 %all-to-all-start.2 = ((f32[16,1,256]{2,1,0:T(1,128)}), f32[16,1,256]{2,1,0:T(1,128)S(1)}, u32[]{:S(2)}, u32[]{:S(2)}) async-start(f32[16,1,256]{2,1,0:T(1,128)} %reshape.482), calls=%async_computation.2 | async-start | bytes 32768 | tf_op jit(solution)/shard_map/all_to_all | solution.py:173
  99.5 2.2 pad_maximum_fusion
  101.8 4.2 all-to-all-done.2
  106.0 4.3 all-to-all-start.3
  111.8 2.5 convolution_convert_fusion.3
  114.3 1.8 reshape.409
  116.1 1.3 fusion.48
  118.8 1.4 reduce.10
  121.8 2.7 all-to-all-done.3
  124.5 2.5 gather_fusion.5
  127.0 1.2 stack_reshape.27
  129.1 2.5 gather_fusion.4
  131.6 1.2 stack_reshape.26
  132.8 0.9 copy.280
  133.7 4.5 fusion.133
  138.2 4.3 copy.247
  142.4 4.1 copy.269
  146.5 9.7 %bitcast_reduce_fusion = (f32[256,4]{0,1:T(4,128)S(1)}, f32[4,256,4096]{2,1,0:T(8,128)}) fusion(bf16[256,4,64]{0,2,1:T(8,128)(2,1)S(1)} %bitcast.204, bf16[4096,4,64]{0,2,1:T(8,128)(2,1)} %bitcast.186), kind=kOutput, calls=%fused_computation.8 | convolution fusion | flops 545258496 | bytes 19009536 | tf_op jit(solution)/shard_map/qhd,khd->qhk/dot_general | solution.py:99
  156.2 8.6 %fusion.2 = f32[256,4]{0,1:T(4,128)S(1)} fusion(f32[4,256,4096]{2,1,0:T(8,128)} %get-tuple-element.35, f32[256,4]{0,1:T(4,128)S(1)} %broadcast_maximum_fusion), kind=kLoop, calls=%fused_computation.11 | loop fusion | flops 12581888 | bytes 16785408 | tf_op jit(solution)/shard_map/reduce_sum | solution.py:104
  164.9 10.2 %fusion.60 = f32[1,256,4,64]{1,3,2,0:T(8,128)} fusion(bf16[4096,4,64]{0,2,1:T(8,128)(2,1)} %bitcast.188, f32[4,256,4096]{2,1,0:T(8,128)} %get-tuple-element.35, f32[256,4]{0,1:T(4,128)S(1)} %broadcast_maximum_fusion, f32[256,4]{0,1:T(4,128)S(1)} %fusion.2), kind=kOutput, calls=%fused_computation.76 | convolution fusion | flops 549519360 | bytes 19144704 | tf_op jit(solution)/shard_map/qhk,khd->qhd/dot_general | solution.py:105
  175.1 1.2 fusion.63
  176.5 1.9 fusion.139
  179.2 65.2 %all-reduce.5.cloned.1.call-done = f32[256,2304]{1,0:T(8,128)} async-done(((f32[256,2304]{1,0:T(8,128)}), f32[256,2304]{1,0:T(8,128)}) %all-reduce.5.cloned.1.call-update) | async-done | bytes 2359312 | tf_op jit(solution)/shard_map/psum | solution.py:188
  244.4 2.1 multiply_reduce_fusion
  246.5 1.4 copy-done.5
  248.0 1.2 convolution_convert_fusion.2
  249.4 66.5 %all-gather.5.cloned.1.call-done = bf16[1536,2304]{1,0:T(8,128)(2,1)} async-done(((bf16[96,2304]{1,0:T(8,128)(2,1)}), bf16[1536,2304]{1,0:T(8,128)(2,1)}) %all-gather.5.cloned.1.call-update) | async-done | bytes 7077904 | tf_op jit(solution)/shard_map/all_gather | solution.py:211
  315.9 7.7 %fusion.36 = f32[1536,360]{0,1:T(8,128)} fusion(bf16[1536,2304]{1,0:T(8,128)(2,1)} %all-gather.5.cloned.1.call-done, bf16[1,2304,360]{1,2,0:T(8,128)(2,1)} %param.37), kind=kOutput, calls=%fused_computation.57 | convolution fusion | flops 2548039680 | bytes 10948608 | tf_op jit(solution)/shard_map/dot_general | solution.py:212
  323.6 14.3 %fusion.33 = f32[1536,2304]{1,0:T(8,128)} fusion(bf16[1,360,2304]{2,1,0:T(8,128)(2,1)S(1)} %copy-done, bf16[1536,2304]{1,0:T(8,128)(2,1)} %all-gather.5.cloned.1.call-done, f32[1536,360]{0,1:T(8,128)} %fusion.36, bf16[1,2304,360]{1,2,0:T(8,128)(2,1)} %param.38), kind=kOutput, calls=%fused_computation.54 | convolution fusion | flops 5099397120 | bytes 26763264 | tf_op jit(solution)/shard_map/dot_general | solution.py:214
  338.7 2.7 fusion.127
  341.5 3.6 gather_fusion.6
  345.5 91.8 %reduce-scatter.3.cloned.1.call-done = f32[96,2304]{1,0:T(8,128)} async-done(((f32[1536,2304]{1,0:T(8,128)}), f32[96,2304]{1,0:T(8,128)}) %reduce-scatter.3.cloned.1.call-update) | async-done | bytes 884752 | tf_op jit(solution)/shard_map/reduce_scatter | solution.py:219
  437.2 3.9 fusion.72
  441.9 29.6 %reduce-scatter.5.cloned.1.call-done = f32[32,2304]{1,0:T(8,128)} async-done(((f32[256,2304]{1,0:T(8,128)}), f32[32,2304]{1,0:T(8,128)}) %reduce-scatter.5.cloned.1.call-update) | async-done | bytes 294928 | tf_op jit(solution)/shard_map/reduce_scatter | solution.py:222
  471.5 1.8 select_convert_fusion
  (159 shorter events, 20.2 us)
Async XLA Ops:
  6.5 317.0 %copy-start = (bf16[1,360,2304]{2,1,0:T(8,128)(2,1)S(1)}, bf16[1,360,2304]{2,1,0:T(8,128)(2,1)}, u32[]{:S(2)}) copy-start(bf16[1,360,2304]{2,1,0:T(8,128)(2,1)} %param.39) | copy-start | bytes 4976644
  6.5 127.2 %all-gather.3.cloned.1.call-start = ((), (), s32[]{:S(2)}) async-start(), calls=%async_computation.6 | async-start | bytes 4456448 | tf_op jit(solution)/shard_map/all_gather | solution.py:94
  9.6 25.4 %all-to-all-start.1 = ((bf16[16,2,32]{2,1,0:T(2,128)(2,1)}), bf16[16,2,32]{2,1,0:T(2,128)(2,1)S(1)}, u32[]{:S(2)}, u32[]{:S(2)}) async-start(bf16[16,2,32]{2,1,0:T(2,128)(2,1)} %broadcast_in_dim.168), calls=%async_computation.1 | async-start | bytes 16384 | tf_op jit(solution)/shard_map/all_to_all | solution.py:156
  19.8 3.6 copy-start.3
  19.8 3.6 copy-start.6
  19.8 3.6 copy-start.38
  19.8 5.5 %copy-start.35 = (f32[256]{0:T(256)}, f32[256]{0:T(256)S(1)}, u32[]{:S(2)}) copy-start(f32[256]{0:T(256)S(1)} %add_rsqrt_fusion.1) | copy-start | bytes 3076
  23.4 3.0 copy-start.2
  27.1 1.1 copy-start.33
  27.1 4.1 copy-start.10
  27.4 4.9 %copy-start.7 = (bf16[2,2,1024,256]{3,2,1,0:T(8,128)(2,1)S(1)}, bf16[2,2,1024,256]{3,2,1,0:T(8,128)(2,1)}, u32[]{:S(2)}) copy-start(bf16[2,2,1024,256]{3,2,1,0:T(8,128)(2,1)} %param.28) | copy-start | bytes 6291460
  29.7 0.8 copy-start.13
  29.7 3.9 copy-start.24
  32.3 1.4 copy-start.32
  35.0 21.3 %all-to-all-start = ((bf16[16,2,32,256]{3,2,1,0:T(8,128)(2,1)}), bf16[16,2,32,256]{3,2,1,0:T(8,128)(2,1)}, u32[]{:S(2)}, u32[]{:S(2)}) async-start(bf16[16,2,32,256]{3,2,1,0:T(8,128)(2,1)} %pad_maximum_fusion.1), calls=%async_computation | async-start | bytes 1048576 | tf_op jit(solution)/shard_map/all_to_all | solution.py:155
  66.7 2.2 copy-start.18
  66.7 2.2 copy-start.16
  66.8 2.2 copy-start.17
  66.8 2.2 copy-start.37
  68.9 2.8 copy-start.20
  78.4 3.2 copy-start.4
  78.4 3.2 copy-start.19
  78.4 3.2 copy-start.21
  78.4 5.5 %copy-start.15 = (bf16[1,1,1024,256]{2,3,1,0:T(8,128)(2,1)S(1)}, bf16[1,1,1024,256]{2,3,1,0:T(8,128)(2,1)}, u32[]{:S(2)}) copy-start(bf16[1,1,1024,256]{2,3,1,0:T(8,128)(2,1)} %copy.270) | copy-start | bytes 1572868
  81.7 0.7 copy-start.22
  88.4 11.1 %copy-start.8 = (f32[16,1,32,256]{3,2,0,1:T(8,128)S(1)}, f32[16,1,32,256]{3,2,0,1:T(8,128)}, u32[]{:S(2)}) copy-start(f32[16,1,32,256]{3,2,0,1:T(8,128)} %stack_reshape.25) | copy-start | bytes 1572868
  92.7 17.7 %copy-start.25 = (f32[8,32,4]{1,2,0:T(4,128)S(1)}, f32[8,32,4]{1,2,0:T(4,128)}, u32[]{:S(2)}) copy-start(f32[8,32,4]{1,2,0:T(4,128)} %copy-done.24) | copy-start | bytes 12292
  92.7 17.7 %copy-start.26 = (f32[8,32,4]{1,2,0:T(4,128)S(1)}, f32[8,32,4]{1,2,0:T(4,128)}, u32[]{:S(2)}) copy-start(f32[8,32,4]{1,2,0:T(4,128)} %fusion.78) | copy-start | bytes 12292
  92.7 19.0 %copy-start.36 = (f32[256]{0:T(256)S(1)}, f32[256]{0:T(256)}, u32[]{:S(2)}) copy-start(f32[256]{0:T(256)} %copy-done.35) | copy-start | bytes 3076
  92.7 13.2 %all-to-all-start.2 = ((f32[16,1,256]{2,1,0:T(1,128)}), f32[16,1,256]{2,1,0:T(1,128)S(1)}, u32[]{:S(2)}, u32[]{:S(2)}) async-start(f32[16,1,256]{2,1,0:T(1,128)} %reshape.482), calls=%async_computation.2 | async-start | bytes 32768 | tf_op jit(solution)/shard_map/all_to_all | solution.py:173
  106.0 4.3 copy-start.27
  106.0 18.6 %all-to-all-start.3 = ((f32[16,2,32,256]{3,2,1,0:T(8,128)}), f32[16,2,32,256]{3,2,1,0:T(8,128)}, u32[]{:S(2)}, u32[]{:S(2)}) async-start(f32[16,2,32,256]{3,2,1,0:T(8,128)} %pad_maximum_fusion), calls=%async_computation.3 | async-start | bytes 2097152 | tf_op jit(solution)/shard_map/all_to_all | solution.py:172
  110.3 5.7 %copy-start.14 = (f32[8,32,4,32]{1,3,2,0:T(8,128)S(1)}, f32[8,32,4,32]{1,3,2,0:T(8,128)}, u32[]{:S(2)}) copy-start(f32[8,32,4,32]{1,3,2,0:T(8,128)} %copy-done.13) | copy-start | bytes 393220
  110.3 134.0 %all-reduce.5.cloned.1.call-start = ((), (), s32[]{:S(2)}) async-start(), calls=%async_computation.7 | async-start | bytes 4718592 | tf_op jit(solution)/shard_map/psum | solution.py:188
  114.3 4.0 copy-start.34
  164.8 10.2 %copy-start.31 = (f32[256,4]{0,1:T(4,128)S(1)}, f32[256,4]{0,1:T(4,128)}, u32[]{:S(2)}) copy-start(f32[256,4]{0,1:T(4,128)} %add.217) | copy-start | bytes 12292
  164.8 10.2 %copy-start.30 = (f32[1,256,4]{1,2,0:T(4,128)S(1)}, f32[1,256,4]{1,2,0:T(4,128)}, u32[]{:S(2)}) copy-start(f32[1,256,4]{1,2,0:T(4,128)} %add.216) | copy-start | bytes 12292
  164.9 10.3 %copy-start.11 = (f32[1,256,4,64]{1,3,2,0:T(8,128)S(1)}, f32[1,256,4,64]{1,3,2,0:T(8,128)}, u32[]{:S(2)}) copy-start(f32[1,256,4,64]{1,3,2,0:T(8,128)} %copy.282) | copy-start | bytes 786436
  164.9 10.3 %copy-start.12 = (f32[1,256,4,64]{1,3,2,0:T(8,128)S(1)}, f32[1,256,4,64]{1,3,2,0:T(8,128)}, u32[]{:S(2)}) copy-start(f32[1,256,4,64]{1,3,2,0:T(8,128)} %copy.281) | copy-start | bytes 786436
  175.1 1.4 copy-start.9
  176.5 2.0 copy-start.29
  178.4 137.5 %all-gather.5.cloned.1.call-start = ((), (), s32[]{:S(2)}) async-start(), calls=%async_computation.8 | async-start | bytes 7520256 | tf_op jit(solution)/shard_map/all_gather | solution.py:211
  179.2 68.8 %copy-start.28 = (f32[2304]{0:T(1024)S(1)}, f32[2304]{0:T(1024)}, u32[]{:S(2)}) copy-start(f32[2304]{0:T(1024)} %param.34) | copy-start | bytes 27652
  246.5 1.5 copy-start.5
  249.2 188.1 %reduce-scatter.3.cloned.1.call-start = ((), (), s32[]{:S(2)}) async-start(), calls=%async_computation.9 | async-start | bytes 15040512 | tf_op jit(solution)/shard_map/reduce_scatter | solution.py:219
  337.9 0.9 copy-start.23
  337.9 133.6 %reduce-scatter.5.cloned.1.call-start = ((), (), s32[]{:S(2)}) async-start(), calls=%async_computation.10 | async-start | bytes 2654208 | tf_op jit(solution)/shard_map/reduce_scatter | solution.py:222
  437.2 36.0 %copy-start.1 = (bf16[1,360,2304]{2,1,0:T(8,128)(2,1)S(1)}, bf16[1,360,2304]{2,1,0:T(8,128)(2,1)}, u32[]{:S(2)}) copy-start(bf16[1,360,2304]{2,1,0:T(8,128)(2,1)} %param.39) | copy-start | bytes 4976644
Sparse Core Ops, SparseCore 0:
  9.6 59.8 all-gather.2
  178.6 65.7 all-reduce.4
  249.3 66.5 all-gather.4
  338.0 99.1 reduce-scatter.2
  441.3 30.1 reduce-scatter.4
where the time goes:
time: 487 us; the launch traced here: 480 us
  waiting for transfers between devices  261 us (54%)
  matrix products  76.3 us (16%)
  local copies, waits for them, and re-layouts  71.6 us (15%)
  other arithmetic  29.4 us (6%)
  starting transfers between devices  27.2 us (6%)
  between operations  14.7 us (3%)
    reduce_scatter x1, waiting for transfers between devices, on_device(): lax.psum_scatter(partial_out, 'dp', scatter_dimension=0, tiled=True)  91.8 us
    all_gather x1, waiting for transfers between devices, on_device(): piece = lax.all_gather(dispatch, 'dp', axis=0, tiled=True)  66.5 us
    psum x1, waiting for transfers between devices, on_device(): attn_all = lax.psum(projected, 'mp')  65.2 us
    reduce_scatter x1, waiting for transfers between devices, on_device(): mixed = lax.psum_scatter(spread, 'mp', scatter_dimension=0, tiled=True)  29.6 us
    dot_general x1, matrix products, on_device(): jnp.dot((jax.nn.silu(gate_part) * up_part).astype(jnp.bfloat16), down_wei...  14.3 us
    unnamed x87, local copies, waits for them, and re-layouts  13.6 us
    dot_general x1, matrix products, on_device(): jnp.einsum('qhk,khd->qhd', weights.astype(jnp.bfloat16), piece_values, pr...  10.2 us
  transfers between devices with their start and end apart: 9, of which 6 were waited for; matrix products, arithmetic and copies ran while one was open for 20% of the time, Pallas kernels for 0%

commit v1 on v0

--- a/solution.py
+++ b/solution.py
@@ -135,7 +135,6 @@
     self_lse = (self_peak + jnp.log(self_total)).reshape(tok_rows, heads_here)
     mid_of = parents[leaf_of]
     leaf_owner = leaf_of // 2
-    leaf_side = (leaf_of % 2).astype(jnp.float32)
     targets = jnp.arange(owners, dtype=jnp.int32)
     pick_mid = (mid_of[None, :] == targets[:, None]).astype(jnp.bfloat16)
     pick_leaf = (leaf_owner[None, :] == targets[:, None]).astype(jnp.bfloat16)
@@ -147,15 +146,11 @@
         jnp.bfloat16
     )
     sent = jnp.stack([sent_mid, sent_leaf], axis=1).reshape(owners, 2, suffix, local_width)
-    side_of_target = jnp.dot(
-        pick_leaf.astype(jnp.float32), leaf_side, precision=lax.Precision.HIGHEST
-    )
-    sides = jnp.stack([jnp.zeros_like(side_of_target), side_of_target], axis=1)
-    sides = jnp.broadcast_to(sides[:, :, None], (owners, 2, suffix)).astype(jnp.bfloat16)
     sent_queries = lax.all_to_all(sent, "dp", split_axis=0, concat_axis=0, tiled=True)
-    sent_sides = lax.all_to_all(sides, "dp", split_axis=0, concat_axis=0, tiled=True)
+    leaf_every = lax.all_gather(leaf_of, "dp", axis=0, tiled=True).reshape(owners, seq_rows)
+    me_dp = lax.axis_index("dp")
+    second = jnp.any((leaf_every // 2 == me_dp) & (leaf_every % 2 == 1), axis=1)
     senders = sent_queries.shape[0]
-    second = sent_sides[:, 1, 0] > 0.5
     mid_limit = jnp.broadcast_to(mid_len[0], (senders,))
     mid_result, mid_logsum = level_partial(
         sent_queries[:, 0], mid_cache[0, 0], mid_cache[1, 0], mid_limit, heads_here, False
@@ -168,10 +163,10 @@
     )
     owner_out = jnp.stack([mid_result, leaf_result], axis=1)
     owner_lse = jnp.stack([mid_logsum, leaf_logsum], axis=1)
-    back_out, back_lse = (
-        lax.all_to_all(owner_out, "dp", split_axis=0, concat_axis=0, tiled=True),
-        lax.all_to_all(owner_lse, "dp", split_axis=0, concat_axis=0, tiled=True),
-    )
+    owner_all = jnp.concatenate([owner_out, owner_lse], axis=-1)
+    back_all = lax.all_to_all(owner_all, "dp", split_axis=0, concat_axis=0, tiled=True)
+    back_out = back_all[..., :local_width]
+    back_lse = back_all[..., local_width:]
     mid_out = back_out[mid_of, 0].reshape(tok_rows, heads_here, head_dim)
     mid_lse = back_lse[mid_of, 0].reshape(tok_rows, heads_here)
     leaf_out = back_out[leaf_owner, 1].reshape(tok_rows, heads_here, head_dim)
@@ -185,10 +180,10 @@
     projected = jnp.dot(attended, w_out, preferred_element_type=jnp.float32)
     rows_here = tok_rows // lax.axis_size("mp")
     first = lax.axis_index("mp") * rows_here
-    attn_all = lax.psum(projected, "mp")
-    resid_all = hidden_in.astype(jnp.float32) + attn_all
-    ffn_in = rms_scale(resid_all, ffn_gain).astype(jnp.bfloat16)
-    resid = lax.dynamic_slice_in_dim(resid_all, first, rows_here, 0)
+    attn_rows = lax.psum_scatter(projected, "mp", scatter_dimension=0, tiled=True)
+    resid = lax.dynamic_slice_in_dim(hidden_in, first, rows_here, 0).astype(jnp.float32) + attn_rows
+    ffn_rows = rms_scale(resid, ffn_gain).astype(jnp.bfloat16)
+    ffn_in = lax.all_gather(ffn_rows, "mp", axis=0, tiled=True)
     logits = jnp.dot(ffn_in.astype(jnp.float32), w_router, precision=lax.Precision.HIGHEST)
     chosen = jnp.take_along_axis(logits, routes, axis=1)
     squashed = jax.nn.sigmoid(chosen)
@@ -216,10 +211,14 @@
         down_weight,
         preferred_element_type=jnp.float32,
     )
-    expert_out = lax.psum_scatter(partial_out, "dp", scatter_dimension=0, tiled=True)
-    weighted = expert_out * slot_gate[:, None]
+    expert_out = lax.psum_scatter(
+        partial_out.astype(jnp.bfloat16), "dp", scatter_dimension=0, tiled=True
+    )
+    weighted = expert_out.astype(jnp.float32) * slot_gate[:, None]
     spread = jnp.dot(pick_slot.astype(jnp.float32).T, weighted, precision=lax.Precision.HIGHEST)
-    mixed = lax.psum_scatter(spread, "mp", scatter_dimension=0, tiled=True)
+    mixed = lax.psum_scatter(
+        spread.astype(jnp.bfloat16), "mp", scatter_dimension=0, tiled=True
+    ).astype(jnp.float32)
     row_ids = first + jnp.arange(rows_here, dtype=jnp.int32)
     valid = row_ids % suffix < suffix_len[row_ids // suffix]
     return jnp.where(valid[:, None], resid + mixed, 0.0).astype(jnp.bfloat16)

time: 487 us -> 444 us (0.912)
  the two profiles are of different devices: /device:TPU:1 before, /device:TPU:0 now
where the time goes in v1:
time: 444 us; the launch traced here: 437 us
  waiting for transfers between devices  237 us (53%)
  matrix products  69.9 us (16%)
  local copies, waits for them, and re-layouts  55.5 us (12%)
  other arithmetic  27.1 us (6%)
  blocking collectives  17.4 us (4%)
  between operations  15.6 us (4%)
  starting transfers between devices  13.8 us (3%)
    reduce_scatter x1, waiting for transfers between devices, on_device(): lax.psum_scatter(partial_out.astype(jnp.bfloat16), 'dp', scatter_dimensio...  76.4 us
    all_gather x1, waiting for transfers between devices, on_device(): piece = lax.all_gather(dispatch, 'dp', axis=0, tiled=True)  65 us
    reduce_scatter x1, waiting for transfers between devices, on_device(): lax.psum_scatter(projected, 'mp', scatter_dimension=0, tiled=True)  31.7 us
    reduce_scatter x1, waiting for transfers between devices, on_device(): lax.psum_scatter(spread.astype(jnp.bfloat16), 'mp', scatter_dimension=0,...  30.7 us
    all_gather x1, waiting for transfers between devices, on_device(): ffn_in = lax.all_gather(ffn_rows, 'mp', axis=0, tiled=True)  21.9 us
    unnamed x1, blocking collectives  17.4 us
    dot_general x1, matrix products, on_device(): jnp.dot((jax.nn.silu(gate_part) * up_part).astype(jnp.bfloat16), down_wei...  13.1 us
    unnamed x64, local copies, waits for them, and re-layouts  11.2 us
  transfers between devices with their start and end apart: 8, of which 6 were waited for; matrix products, arithmetic and copies ran while one was open for 18% of the time, Pallas kernels for 0%

profile of v1, /device:TPU:0, one launch (start us, length us, event | category | flops | bytes accessed | tf_op | source)
XLA Modules:
  0.0 436.8 jit_solution(13475134126374077228)
XLA Ops:
  7.3 1.6 fusion.30
  9.6 2.4 convolution_convert_fusion.7
  14.0 0.9 pad_maximum_fusion.1
  14.9 8.2 %all-to-all-start = ((bf16[16,2,32,256]{3,2,1,0:T(8,128)(2,1)}), bf16[16,2,32,256]{3,2,1,0:T(8,128)(2,1)}, u32[]{:S(2)}, u32[]{:S(2)}) async-start(bf16[16,2,32,256]{3,2,1,0:T(8,128)(2,1)} %pad_maximum_fusion.1), calls=%async_computation | async-start | bytes 1048576 | tf_op jit(solution)/shard_map/all_to_all | solution.py:149
  24.6 17.4 %all-reduce.2 = s32[128]{0:T(128)S(1)} all-reduce(s32[128]{0:T(128)S(1)} %dynamic-update-slice), channel_id=1, replica_groups=mesh['dp'=16,'mp'=8] {'dp'}, use_global_device_ids=true, to_apply=%add.2 | all-reduce | flops 128 | bytes 1024
  42.9 1.3 broadcast_select_fusion
  44.9 2.2 fusion.126
  47.2 2.5 convolution_convert_fusion.6
  49.7 1.2 fusion.125
  50.8 0.9 reshape.404
  51.7 0.9 reshape.403
  52.6 1.0 copy.259
  53.8 2.1 copy.294
  56.0 2.1 copy.296
  58.1 1.0 copy.295
  59.1 1.0 copy.297
  60.2 2.0 fusion.129
  62.2 1.1 fusion.127
  63.3 1.0 reshape_squeeze.19
  64.6 4.3 bitcast_reduce_fusion.1
  68.9 2.6 fusion.15
  71.6 2.7 fusion.58
  75.1 1.4 stack_reshape.23
  76.5 2.4 bitcast_reduce_fusion.2
  78.9 2.0 fusion.13
  80.9 1.8 fusion.63
  83.5 1.4 stack_reshape.22
  85.2 2.4 pad_maximum_fusion
  87.6 5.1 %all-to-all-start.1 = ((f32[16,2,32,260]{3,2,1,0:T(8,128)}), f32[16,2,32,260]{3,2,1,0:T(8,128)S(1)}, u32[]{:S(2)}, u32[]{:S(2)}) async-start(f32[16,2,32,260]{3,2,1,0:T(8,128)} %pad_maximum_fusion), calls=%async_computation.1 | async-start | bytes 3145728 | tf_op jit(solution)/shard_map/all_to_all | solution.py:167
  92.9 1.2 fusion.74
  94.3 2.8 convolution_convert_fusion.5
  97.1 1.1 reshape.405
  98.2 1.4 fusion.45
  99.6 0.9 copy.285
  100.4 1.9 copy.288
  102.3 10.9 %all-to-all-done.1 = f32[16,2,32,260]{3,2,1,0:T(8,128)S(1)} async-done(((f32[16,2,32,260]{3,2,1,0:T(8,128)}), f32[16,2,32,260]{3,2,1,0:T(8,128)S(1)}, u32[]{:S(2)}, u32[]{:S(2)}) %all-to-all-start.1) | async-done | bytes 1064992 | tf_op jit(solution)/shard_map/all_to_all | solution.py:167
  113.2 0.8 slice.82
  114.1 1.3 copy.298
  116.9 1.1 slice.84
  118.0 1.8 gather_fusion.4
  119.8 1.8 gather_fusion.5
  122.5 4.5 %fusion.124 = (bf16[1,4096,256]{2,1,0:T(8,128)(2,1)}, bf16[1,4096,256]{2,1,0:T(8,128)(2,1)}) fusion(bf16[2,4096,256]{2,1,0:T(8,128)(2,1)} %all-gather.4.cloned.1.call-done), kind=kLoop, calls=%fused_computation.185 | loop fusion | bytes 8388608 | tf_op jit(solution)/shard_map/slice | solution.py:96
  127.0 4.1 copy.253
  131.1 4.2 copy.282
  135.2 9.7 %bitcast_reduce_fusion = (f32[256,4]{0,1:T(4,128)S(1)}, f32[4,256,4096]{2,1,0:T(8,128)}) fusion(bf16[256,4,64]{0,2,1:T(8,128)(2,1)S(1)} %bitcast.190, bf16[4096,4,64]{0,2,1:T(8,128)(2,1)} %bitcast.174), kind=kOutput, calls=%fused_computation.8 | convolution fusion | flops 545258496 | bytes 19009536 | tf_op jit(solution)/shard_map/qhd,khd->qhk/dot_general | solution.py:99
  144.9 8.6 %fusion.2 = f32[256,4]{0,1:T(4,128)S(1)} fusion(f32[4,256,4096]{2,1,0:T(8,128)} %get-tuple-element.33, f32[256,4]{0,1:T(4,128)S(1)} %broadcast_maximum_fusion), kind=kLoop, calls=%fused_computation.11 | loop fusion | flops 12581888 | bytes 16785408 | tf_op jit(solution)/shard_map/reduce_sum | solution.py:104
  153.6 8.1 %fusion.54 = f32[1,256,4,64]{1,3,2,0:T(8,128)S(1)} fusion(bf16[4096,4,64]{0,2,1:T(8,128)(2,1)} %bitcast.176, f32[4,256,4096]{2,1,0:T(8,128)} %get-tuple-element.33, f32[256,4]{0,1:T(4,128)S(1)} %broadcast_maximum_fusion, f32[256,4]{0,1:T(4,128)S(1)} %fusion.2), kind=kOutput, calls=%fused_computation.71 | convolution fusion | flops 549519360 | bytes 19144704 | tf_op jit(solution)/shard_map/qhk,khd->qhd/dot_general | solution.py:105
  161.9 1.1 copy-done.11
  163.0 1.9 fusion.130
  165.0 31.7 %reduce-scatter.4.cloned.1.call-done = f32[32,2304]{1,0:T(8,128)} async-done(((f32[256,2304]{1,0:T(8,128)}), f32[32,2304]{1,0:T(8,128)}) %reduce-scatter.4.cloned.1.call-update) | async-done | bytes 294928 | tf_op jit(solution)/shard_map/reduce_scatter | solution.py:183
  196.6 1.1 multiply_reduce_fusion
  197.8 1.8 multiply_convert_fusion
  200.3 21.9 %all-gather.6.cloned.1.call-done = bf16[256,2304]{1,0:T(8,128)(2,1)} async-done(((bf16[32,2304]{1,0:T(8,128)(2,1)}), bf16[256,2304]{1,0:T(8,128)(2,1)}) %all-gather.6.cloned.1.call-update) | async-done | bytes 1179664 | tf_op jit(solution)/shard_map/all_gather | solution.py:186
  222.2 2.4 convolution_convert_fusion.4
  224.9 65.0 %all-gather.8.cloned.1.call-done = bf16[1536,2304]{1,0:T(8,128)(2,1)} async-done(((bf16[96,2304]{1,0:T(8,128)(2,1)}), bf16[1536,2304]{1,0:T(8,128)(2,1)}) %all-gather.8.cloned.1.call-update) | async-done | bytes 7077904 | tf_op jit(solution)/shard_map/all_gather | solution.py:206
  289.9 7.6 %fusion.35 = f32[1536,360]{0,1:T(8,128)} fusion(bf16[1536,2304]{1,0:T(8,128)(2,1)} %all-gather.8.cloned.1.call-done, bf16[1,2304,360]{1,2,0:T(8,128)(2,1)} %param.37), kind=kOutput, calls=%fused_computation.55 | convolution fusion | flops 2548039680 | bytes 10948608 | tf_op jit(solution)/shard_map/dot_general | solution.py:207
  297.5 13.1 %convolution_convert_fusion = bf16[1536,2304]{1,0:T(8,128)(2,1)} fusion(bf16[1,360,2304]{2,1,0:T(8,128)(2,1)S(1)} %copy-done, bf16[1536,2304]{1,0:T(8,128)(2,1)} %all-gather.8.cloned.1.call-done, f32[1536,360]{0,1:T(8,128)} %fusion.35, bf16[1,2304,360]{1,2,0:T(8,128)(2,1)} %param.38), kind=kOutput, calls=%fused_computation.12 | convolution fusion | flops 5102936064 | bytes 19685376 | tf_op jit(solution)/shard_map/dot_general | solution.py:209
  311.0 0.9 copy-done.4
  311.9 1.0 fusion.131
  312.9 3.6 gather_fusion.6
  316.9 76.4 %reduce-scatter.6.cloned.1.call-done = bf16[96,2304]{1,0:T(8,128)(2,1)} async-done(((bf16[1536,2304]{1,0:T(8,128)(2,1)}), bf16[96,2304]{1,0:T(8,128)(2,1)}) %reduce-scatter.6.cloned.1.call-update) | async-done | bytes 442384 | tf_op jit(solution)/shard_map/reduce_scatter | solution.py:214
  393.3 3.2 convolution_convert_fusion.3
  397.3 30.7 %reduce-scatter.8.cloned.1.call-done = bf16[32,2304]{1,0:T(8,128)(2,1)} async-done(((bf16[256,2304]{1,0:T(8,128)(2,1)}), bf16[32,2304]{1,0:T(8,128)(2,1)}) %reduce-scatter.8.cloned.1.call-update) | async-done | bytes 147472 | tf_op jit(solution)/shard_map/reduce_scatter | solution.py:219
  428.0 1.7 select_convert_fusion
  (135 shorter events, 13.1 us)
Async XLA Ops:
  6.5 290.9 %copy-start = (bf16[1,360,2304]{2,1,0:T(8,128)(2,1)S(1)}, bf16[1,360,2304]{2,1,0:T(8,128)(2,1)}, u32[]{:S(2)}) copy-start(bf16[1,360,2304]{2,1,0:T(8,128)(2,1)} %param.39) | copy-start | bytes 4976644
  6.5 116.0 %all-gather.4.cloned.1.call-start = ((), (), s32[]{:S(2)}) async-start(), calls=%async_computation.5 | async-start | bytes 4456448 | tf_op jit(solution)/shard_map/all_gather | solution.py:94
  9.5 3.5 copy-start.2
  11.9 0.7 copy-start.16
  12.7 10.4 %copy-start.26 = (u32[128]{0:T(128)S(1)}, u32[128]{0:T(128)}, u32[]{:S(2)}) copy-start(u32[128]{0:T(128)} %constant.214) | copy-start | bytes 1540
  12.7 11.7 %copy-start.24 = (s32[8]{0:T(128)S(1)}, s32[8]{0:T(128)}, u32[]{:S(2)}) copy-start(s32[8]{0:T(128)} %param.31) | copy-start | bytes 100
  12.7 29.3 %copy-start.3 = (s32[8]{0:T(128)S(1)}, s32[8]{0:T(128)}, u32[]{:S(2)}) copy-start(s32[8]{0:T(128)} %param.33) | copy-start | bytes 100
  12.7 29.3 %copy-start.23 = (s32[2]{0:T(128)S(1)}, s32[2]{0:T(128)}, u32[]{:S(2)}) copy-start(s32[2]{0:T(128)} %param.30) | copy-start | bytes 28
  14.0 33.2 %copy-start.6 = (bf16[256,2304]{1,0:T(8,128)(2,1)S(1)}, bf16[256,2304]{1,0:T(8,128)(2,1)}, u32[]{:S(2)}) copy-start(bf16[256,2304]{1,0:T(8,128)(2,1)} %param.20) | copy-start | bytes 3538948
  14.9 47.3 %all-to-all-start = ((bf16[16,2,32,256]{3,2,1,0:T(8,128)(2,1)}), bf16[16,2,32,256]{3,2,1,0:T(8,128)(2,1)}, u32[]{:S(2)}, u32[]{:S(2)}) async-start(bf16[16,2,32,256]{3,2,1,0:T(8,128)(2,1)} %pad_maximum_fusion.1), calls=%async_computation | async-start | bytes 1048576 | tf_op jit(solution)/shard_map/all_to_all | solution.py:149
  44.9 4.7 %copy-start.7 = (bf16[2,2,1024,256]{3,2,1,0:T(8,128)(2,1)S(1)}, bf16[2,2,1024,256]{3,2,1,0:T(8,128)(2,1)}, u32[]{:S(2)}) copy-start(bf16[2,2,1024,256]{3,2,1,0:T(8,128)(2,1)} %param.28) | copy-start | bytes 6291460
  49.7 2.1 copy-start.19
  49.7 3.9 copy-start.9
  53.8 4.2 copy-start.10
  53.8 6.4 %copy-start.18 = (bf16[8,32,4,64]{3,2,1,0:T(4,128)(2,1)S(1)}, bf16[8,32,4,64]{3,2,1,0:T(4,128)(2,1)}, u32[]{:S(2)}) copy-start(bf16[8,32,4,64]{3,2,1,0:T(4,128)(2,1)} %reshape.404) | copy-start | bytes 393220
  68.9 2.7 copy-start.14
  68.9 2.7 copy-start.15
  78.9 2.0 copy-start.13
  82.8 2.5 copy-start.8
  87.6 6.6 %copy-start.25 = (f32[2304]{0:T(1024)S(1)}, f32[2304]{0:T(1024)}, u32[]{:S(2)}) copy-start(f32[2304]{0:T(1024)} %param.21) | copy-start | bytes 27652
  87.6 25.6 %all-to-all-start.1 = ((f32[16,2,32,260]{3,2,1,0:T(8,128)}), f32[16,2,32,260]{3,2,1,0:T(8,128)S(1)}, u32[]{:S(2)}, u32[]{:S(2)}) async-start(f32[16,2,32,260]{3,2,1,0:T(8,128)} %pad_maximum_fusion), calls=%async_computation.1 | async-start | bytes 3145728 | tf_op jit(solution)/shard_map/all_to_all | solution.py:167
  92.7 104.0 %reduce-scatter.4.cloned.1.call-start = ((), (), s32[]{:S(2)}) async-start(), calls=%async_computation.6 | async-start | bytes 2654208 | tf_op jit(solution)/shard_map/reduce_scatter | solution.py:183
  131.1 4.2 copy-start.17
  153.6 8.2 %copy-start.12 = (f32[1,256,4,64]{1,3,2,0:T(8,128)S(1)}, f32[1,256,4,64]{1,3,2,0:T(8,128)}, u32[]{:S(2)}) copy-start(f32[1,256,4,64]{1,3,2,0:T(8,128)} %copy.288) | copy-start | bytes 786436
  161.7 1.3 copy-start.11
  163.0 34.8 %copy-start.22 = (f32[2304]{0:T(1024)S(1)}, f32[2304]{0:T(1024)}, u32[]{:S(2)}) copy-start(f32[2304]{0:T(1024)} %param.34) | copy-start | bytes 27652
  164.9 34.8 %copy-start.21 = (s32[256,2]{0,1:T(2,128)S(1)}, s32[256,2]{0,1:T(2,128)}, u32[]{:S(2)}) copy-start(s32[256,2]{0,1:T(2,128)} %param.36) | copy-start | bytes 6148
  164.9 57.3 %all-gather.6.cloned.1.call-start = ((), (), s32[]{:S(2)}) async-start(), calls=%async_computation.7 | async-start | bytes 1327104 | tf_op jit(solution)/shard_map/all_gather | solution.py:186
  199.6 90.3 %all-gather.8.cloned.1.call-start = ((), (), s32[]{:S(2)}) async-start(), calls=%async_computation.8 | async-start | bytes 7520256 | tf_op jit(solution)/shard_map/all_gather | solution.py:206
  224.6 168.7 %reduce-scatter.6.cloned.1.call-start = ((), (), s32[]{:S(2)}) async-start(), calls=%async_computation.9 | async-start | bytes 7520256 | tf_op jit(solution)/shard_map/reduce_scatter | solution.py:214
  310.6 1.3 copy-start.4
  310.6 1.3 copy-start.20
  310.6 117.3 %reduce-scatter.8.cloned.1.call-start = ((), (), s32[]{:S(2)}) async-start(), calls=%async_computation.10 | async-start | bytes 1327104 | tf_op jit(solution)/shard_map/reduce_scatter | solution.py:219
  312.9 116.8 %copy-start.1 = (bf16[1,360,2304]{2,1,0:T(8,128)(2,1)S(1)}, bf16[1,360,2304]{2,1,0:T(8,128)(2,1)}, u32[]{:S(2)}) copy-start(bf16[1,360,2304]{2,1,0:T(8,128)(2,1)} %param.39) | copy-start | bytes 4976644
  316.4 111.5 %copy-start.5 = (f32[32,2304]{1,0:T(8,128)S(1)}, f32[32,2304]{1,0:T(8,128)}, u32[]{:S(2)}) copy-start(f32[32,2304]{1,0:T(8,128)} %reduce-scatter.4.cloned.1.call-done) | copy-start | bytes 884740
Sparse Core Ops, SparseCore 0:
  9.6 57.6 all-gather.3
  165.0 31.5 reduce-scatter.3
  199.7 22.4 all-gather.5
  224.7 65.1 all-gather.7
  310.8 82.4 reduce-scatter.5
  396.6 31.2 reduce-scatter.7
